TPU v7x, 32 devices: a whole 2x2x4 slice. The times are simulated.
32 devices in a mesh: row: 4 (over z), col: 2 (over x), depth: 4 (over y, core).
Axes of the slice: x: 2, y: 2, z: 4, core: 2. Of those that a mesh axis runs over, the one named last changes fastest.
Arguments:
- tokens: bfloat16 [2560, 8192], P(('row', 'depth'), 'col'), may hold values from -6 to 6
- weight: bfloat16 [8192, 4096], P('row', 'col'), may hold values from -0.0625 to 0.0625
- cotangent: bfloat16 [2560, 4096], P(('row', 'depth'), 'col'), may hold values from -6 to 6
- master: float32 [8192, 4096], P(('row', 'depth'), 'col'), may hold values from -0.1 to 0.1
- first_moment: float32 [8192, 4096], P(('row', 'depth'), 'col'), may hold values from -6 to 6
- second_moment: float32 [8192, 4096], P(('row', 'depth'), 'col'), may hold values from 0.1 to 10
Outputs:
- queries: bfloat16 [2560, 4096], P(('row', 'depth'), 'col')
- token_grad: bfloat16 [2560, 8192], P(('row', 'depth'), 'col')
- new_master: float32 [8192, 4096], P(('row', 'depth'), 'col')
- new_first: float32 [8192, 4096], P(('row', 'depth'), 'col')
- new_second: float32 [8192, 4096], P(('row', 'depth'), 'col')
- new_weight: bfloat16 [8192, 4096], P('row', 'col')
All inputs are finite; a program needn't handle non-finite values.
Results may differ from a plain program's by a relative error of at most 0.001.
Values may be sent and summed in bfloat16 or wider, within the bound.
A program may use at most 128 MiB of HBM per device.

v0:
```python
import math

import jax
import jax.numpy as jnp
from jax import lax
from jax.sharding import PartitionSpec as P


beta_one = 0.9
beta_two = 0.95
learn_rate = 0.02
decay_rate = 0.1
adam_eps = 1e-08
bias_one = 1.0 - 0.9**50
bias_two = 1.0 - 0.95**50


def swap(value, axis, step):
    size = lax.axis_size(axis)
    return lax.ppermute(value, axis, [(i, i ^ step) for i in range(size)])


def spread(value, axis):
    pieces = [value]
    for step in range(1, lax.axis_size(axis)):
        top = 1 << (step.bit_length() - 1)
        low = step & -step
        pieces.append(swap(pieces[step - low], axis, low) if step != top else swap(value, axis, step))
    return pieces


def exchange(value, axis, dim, width):
    me = lax.axis_index(axis)
    pieces = []
    for step in range(lax.axis_size(axis)):
        piece = lax.dynamic_slice_in_dim(value, (me ^ step) * width, width, dim)
        pieces.append(swap(piece, axis, step) if step else piece)
    return pieces


def in_order(pieces, axis, dim):
    me = lax.axis_index(axis)
    size = pieces[0].shape[dim]
    shape = list(pieces[0].shape)
    shape[dim] = size * len(pieces)
    whole = jnp.zeros(shape, pieces[0].dtype)
    for step, piece in enumerate(pieces):
        whole = lax.dynamic_update_slice_in_dim(whole, piece, (me ^ step) * size, dim)
    return whole


def step(tokens, weight, cotangent, master, first_moment, second_moment):
    rows, cols, depths = lax.axis_size("row"), lax.axis_size("col"), lax.axis_size("depth")
    col_at = lax.axis_index("col")
    block = tokens.shape[0]
    total_tokens = block * rows * depths
    grad_scale = 1.0 / math.sqrt(total_tokens)
    full_rows = in_order(spread(tokens, "col"), "col", 1)
    line_cotangent = lax.all_gather(cotangent, "row", axis=0, tiled=True)
    line_pieces = exchange(full_rows, "row", 1, weight.shape[0])
    features = weight.shape[0] // cols
    parts = []
    for step in reversed(range(cols)):
        panel = lax.dynamic_slice_in_dim(weight, (col_at ^ step) * features, features, 0)
        part = lax.dot_general(
            line_cotangent, panel, (((1,), (1,)), ((), ())), preferred_element_type=jnp.float32
        )
        parts.append(swap(part, "col", step) if step else part)
    piece = sum(parts[1:], parts[0]).astype(jnp.bfloat16)
    line_tokens = in_order(line_pieces, "row", 0)
    partial_queries = jnp.dot(line_tokens, weight, preferred_element_type=jnp.float32)
    queries = lax.psum_scatter(partial_queries, "row", scatter_dimension=0, tiled=True).astype(
        jnp.bfloat16
    )
    piece = in_order(exchange(piece, "row", 0, block), "row", 0)
    piece = in_order(exchange(piece, "col", 0, block * rows // cols), "col", 0)
    piece = piece.reshape(cols, rows // cols, block, -1)
    token_grad = piece.transpose(2, 1, 0, 3).reshape(tokens.shape)
    shard = line_tokens.shape[1] // depths
    product = 0.0
    slabs = exchange(line_tokens, "depth", 1, shard)
    cotangents = spread(line_cotangent, "depth")
    for slab, other_cotangent in zip(slabs, cotangents):
        product = product + lax.dot_general(
            slab, other_cotangent, (((0,), (0,)), ((), ())), preferred_element_type=jnp.float32
        )
    grad = product * grad_scale
    new_first = beta_one * first_moment + (1.0 - beta_one) * grad
    new_second = beta_two * second_moment + (1.0 - beta_two) * grad * grad
    step_value = new_first / bias_one / (jnp.sqrt(new_second / bias_two) + adam_eps)
    new_master = master - learn_rate * (step_value + decay_rate * master)
    shard_weight = new_master.astype(jnp.bfloat16)
    new_weight = in_order(spread(shard_weight, "depth"), "depth", 0)
    return (queries, token_grad, new_master, new_first, new_second, new_weight)


def solution(mesh):
    in_specs = (
        P(("row", "depth"), "col"),
        P("row", "col"),
        P(("row", "depth"), "col"),
        P(("row", "depth"), "col"),
        P(("row", "depth"), "col"),
        P(("row", "depth"), "col"),
    )
    out_specs = (
        P(("row", "depth"), "col"),
        P(("row", "depth"), "col"),
        P(("row", "depth"), "col"),
        P(("row", "depth"), "col"),
        P(("row", "depth"), "col"),
        P("row", "col"),
    )
    return jax.shard_map(step, mesh=mesh, in_specs=in_specs, out_specs=out_specs, check_vma=False)
```

profile of v0, /device:TPU:0, one launch (start us, length us, event | category | flops | bytes accessed | tf_op | source)
XLA Modules:
  0.0 360.1 jit_solution(10849362117627997346)
XLA Ops:
  8.0 3.0 collective-permute-start
  11.4 28.5 %collective-permute-done = bf16[160,4096]{1,0:T(8,128)(2,1)S(1)} collective-permute-done((bf16[160,4096]{1,0:T(8,128)(2,1)}, bf16[160,4096]{1,0:T(8,128)(2,1)S(1)}, u32[]{:S(2)}, u32[]{:S(2)}) %collective-permute-start) | collective-permute-done | bytes 1310752 | tf_op jit(solution)/shard_map/ppermute | solution.py:20
  41.7 1.8 collective-permute-start.1
  43.6 2.6 collective-permute-start.2
  46.2 47.0 %collective-permute-done.1 = bf16[160,2048]{1,0:T(8,128)(2,1)} collective-permute-done((bf16[160,2048]{1,0:T(8,128)(2,1)}, bf16[160,2048]{1,0:T(8,128)(2,1)}, u32[]{:S(2)}, u32[]{:S(2)}) %collective-permute-start.1) | collective-permute-done | bytes 655392 | tf_op jit(solution)/shard_map/ppermute | solution.py:20
  95.4 13.9 %collective-permute-done.3 = bf16[160,2048]{1,0:T(8,128)(2,1)} collective-permute-done((bf16[160,2048]{1,0:T(8,128)(2,1)S(1)}, bf16[160,2048]{1,0:T(8,128)(2,1)}, u32[]{:S(2)}, u32[]{:S(2)}) %collective-permute-start.3) | collective-permute-done | bytes 655392 | tf_op jit(solution)/shard_map/ppermute | solution.py:20
  110.5 1.5 collective-permute-start.12
  112.0 9.5 %fusion.15 = f32[640,2048]{1,0:T(8,128)} fusion(bf16[640,2048]{1,0:T(8,128)(2,1)S(1)} %constant_dynamic-update-slice_fusion.8, bf16[2048,2048]{1,0:T(8,128)(2,1)} %param.7), kind=kOutput, calls=%fused_computation.43 | convolution fusion | flops 5368709120 | bytes 16252928 | tf_op jit(solution)/shard_map/dot_general | solution.py:71
  121.6 47.5 %collective-permute-done.12 = bf16[640,2048]{1,0:T(8,128)(2,1)} collective-permute-done((bf16[640,2048]{1,0:T(8,128)(2,1)}, bf16[640,2048]{1,0:T(8,128)(2,1)}, u32[]{:S(2)}, u32[]{:S(2)}) %collective-permute-start.12) | collective-permute-done | bytes 2621472 | tf_op jit(solution)/shard_map/ppermute | solution.py:20
  169.4 1.7 collective-permute-start.13
  171.6 7.3 %fusion.5 = f32[640,1024]{0,1:T(8,128)} fusion(bf16[640,2048]{1,0:T(8,128)(2,1)S(1)} %copy-done, bf16[2048,2048]{1,0:T(8,128)(2,1)} %param.7, s32[]{:T(128)S(6)} %select_n.78), kind=kOutput, calls=%fused_computation.10 | convolution fusion | flops 2684354560 | bytes 9437188 | tf_op jit(solution)/shard_map/dot_general | solution.py:65
  178.8 3.9 %fusion.10 = f32[512,2048]{1,0:T(8,128)} fusion(bf16[640,2048]{1,0:T(8,128)(2,1)S(1)} %copy-done, bf16[640,2048]{1,0:T(8,128)(2,1)S(1)} %constant_dynamic-update-slice_fusion.8, s32[]{:T(128)S(6)} %select_n.82), kind=kOutput, calls=%fused_computation.12 | convolution fusion | flops 1342177280 | bytes 7471108 | tf_op jit(solution)/shard_map/dot_general | solution.py:84
  182.8 17.7 %collective-permute-done.11 = bf16[640,512]{1,0:T(8,128)(2,1)S(1)} collective-permute-done((bf16[640,512]{1,0:T(8,128)(2,1)S(1)}, bf16[640,512]{1,0:T(8,128)(2,1)S(1)}, u32[]{:S(2)}, u32[]{:S(2)}) %collective-permute-start.11) | collective-permute-done | bytes 655392 | tf_op jit(solution)/shard_map/ppermute | solution.py:20
  202.0 3.6 fusion.17
  205.6 3.6 fusion.16
  210.0 4.5 %broadcast_in_dim.11 = bf16[2048,2048]{1,0:T(8,128)(2,1)} broadcast(bf16[]{:T(256)} %constant.26.clone.1), dimensions={} | broadcast | bytes 8388610 | tf_op jit(solution)/shard_map/broadcast_in_dim | solution.py:46
  214.5 14.3 %constant_dynamic-update-slice_fusion.1 = (bf16[2048,2048]{1,0:T(8,128)(2,1)}, bf16[512,2048]{1,0:T(8,128)(2,1)}, f32[512,2048]{1,0:T(8,128)}, f32[512,2048]{1,0:T(8,128)}, f32[512,2048]{1,0:T(8,128)}) fusion(bf16[2048,2048]{1,0:T(8,128)(2,1)} %broadcast_in_dim.11, s32[]{:T(128)S(6)} %select_n.82, f32[512,2048]{1,0:T(8,128)} %param.9, ...), kind=kOutput, calls=%fused_computation.16 | convolution fusion | flops 1363148800 | bytes 45219844 | tf_op jit(solution)/shard_map/dot_general | solution.py:84
  228.8 1.5 collective-permute-start.16
  230.3 28.8 %collective-permute-done.4 = f32[640,1024]{0,1:T(8,128)} collective-permute-done((f32[640,1024]{0,1:T(8,128)}, f32[640,1024]{0,1:T(8,128)}, u32[]{:S(2)}, u32[]{:S(2)}) %collective-permute-start.4) | collective-permute-done | bytes 2621472 | tf_op jit(solution)/shard_map/ppermute | solution.py:20
  259.1 6.5 %fusion.4 = bf16[640,1024]{0,1:T(8,128)(2,1)S(1)} fusion(f32[640,1024]{0,1:T(8,128)} %collective-permute-done.4, bf16[640,2048]{1,0:T(8,128)(2,1)S(1)} %copy-done.1, bf16[2048,2048]{1,0:T(8,128)(2,1)} %param.7, s32[]{:T(128)S(6)} %select_n.79), kind=kOutput, calls=%fused_computation.9 | convolution fusion | flops 2685665280 | bytes 10747908 | tf_op jit(solution)/shard_map/dot_general | solution.py:65
  265.7 2.2 constant_dynamic-slice_fusion.4
  268.2 15.5 %collective-permute-start.6 = (bf16[160,1024]{0,1:T(8,128)(2,1)}, bf16[160,1024]{0,1:T(8,128)(2,1)}, u32[]{:S(2)}, u32[]{:S(2)}) collective-permute-start(bf16[160,1024]{0,1:T(8,128)(2,1)} %get-tuple-element.21), channel_id=1, source_target_pairs={{0,16},{8,24},{16,0},{24,8},{1,17},{9,25},{17,1},{25,9},{2,18},{10... | collective-permute-start | bytes 983048 | tf_op jit(solution)/shard_map/ppermute | solution.py:20
  285.9 2.0 copy.23
  287.8 29.2 %collective-permute-done.6 = bf16[160,1024]{0,1:T(8,128)(2,1)} collective-permute-done((bf16[160,1024]{0,1:T(8,128)(2,1)}, bf16[160,1024]{0,1:T(8,128)(2,1)}, u32[]{:S(2)}, u32[]{:S(2)}) %collective-permute-start.6) | collective-permute-done | bytes 327712 | tf_op jit(solution)/shard_map/ppermute | solution.py:20
  317.0 1.9 copy.22
  319.0 1.9 copy.21
  324.2 1.5 collective-permute-start.8
  325.7 14.3 %collective-permute-done.8 = bf16[320,1024]{1,0:T(8,128)(2,1)S(1)} collective-permute-done((bf16[320,1024]{1,0:T(8,128)(2,1)S(1)}, bf16[320,1024]{1,0:T(8,128)(2,1)S(1)}, u32[]{:S(2)}, u32[]{:S(2)}) %collective-permute-start.8) | collective-permute-done | bytes 655392 | tf_op jit(solution)/shard_map/ppermute | solution.py:20
  341.4 1.8 reshape.19
  343.2 3.2 constant_dynamic-update-slice_fusion
  346.4 3.2 constant_dynamic-update-slice_fusion.11
  349.6 2.2 convert_element_type.9
  (54 shorter events, 18.1 us)
Async XLA Ops:
  7.2 4.1 %copy-start.2 = (bf16[160,4096]{1,0:T(8,128)(2,1)S(1)}, bf16[160,4096]{1,0:T(8,128)(2,1)}, u32[]{:S(2)}) copy-start(bf16[160,4096]{1,0:T(8,128)(2,1)} %param.6) | copy-start | bytes 3932164
  7.2 103.3 %all-gather.2.cloned.1.call-start = ((), (), s32[]{:S(2)}) async-start(), calls=%async_computation.2 | async-start | bytes 3276800 | tf_op jit(solution)/shard_map/all_gather | solution.py:59
  7.9 341.7 %reduce-scatter.2.cloned.1.call-start = ((), (), s32[]{:S(2)}) async-start(), calls=%async_computation.1 | async-start | bytes 6553600 | tf_op jit(solution)/shard_map/reduce_scatter | solution.py:72
  8.0 32.0 %collective-permute-start = (bf16[160,4096]{1,0:T(8,128)(2,1)}, bf16[160,4096]{1,0:T(8,128)(2,1)S(1)}, u32[]{:S(2)}, u32[]{:S(2)}) collective-permute-start(bf16[160,4096]{1,0:T(8,128)(2,1)} %param.6), channel_id=1, source_target_pairs={{0,4},{4,0},{1,5},{5,1},{2,6},{6,2},{3,7},{7,3},{8,12},{12,8},{9,1... | collective-permute-start | bytes 3932168 | tf_op jit(solution)/shard_map/ppermute | solution.py:20
  41.7 51.4 %collective-permute-start.1 = (bf16[160,2048]{1,0:T(8,128)(2,1)}, bf16[160,2048]{1,0:T(8,128)(2,1)}, u32[]{:S(2)}, u32[]{:S(2)}) collective-permute-start(bf16[160,2048]{1,0:T(8,128)(2,1)} %get-tuple-element.16), channel_id=1, source_target_pairs={{0,8},{8,0},{16,24},{24,16},{1,9},{9,1},{17,25},{25,17},{2,10},{10... | collective-permute-start | bytes 1966088 | tf_op jit(solution)/shard_map/ppermute | solution.py:20
  43.6 50.7 %collective-permute-start.2 = (bf16[160,2048]{1,0:T(8,128)(2,1)}, bf16[160,2048]{1,0:T(8,128)(2,1)}, u32[]{:S(2)}, u32[]{:S(2)}) collective-permute-start(bf16[160,2048]{1,0:T(8,128)(2,1)} %get-tuple-element.15), channel_id=1, source_target_pairs={{0,16},{8,24},{16,0},{24,8},{1,17},{9,25},{17,1},{25,9},{2,18},{10... | collective-permute-start | bytes 1966088 | tf_op jit(solution)/shard_map/ppermute | solution.py:20
  46.2 63.1 %collective-permute-start.3 = (bf16[160,2048]{1,0:T(8,128)(2,1)S(1)}, bf16[160,2048]{1,0:T(8,128)(2,1)}, u32[]{:S(2)}, u32[]{:S(2)}) collective-permute-start(bf16[160,2048]{1,0:T(8,128)(2,1)S(1)} %get-tuple-element.14), channel_id=1, source_target_pairs={{0,24},{8,16},{16,8},{24,0},{1,25},{9,17},{17,9},{25,1},{2,26},{10... | collective-permute-start | bytes 1966088 | tf_op jit(solution)/shard_map/ppermute | solution.py:20
  110.5 58.6 %collective-permute-start.12 = (bf16[640,2048]{1,0:T(8,128)(2,1)}, bf16[640,2048]{1,0:T(8,128)(2,1)}, u32[]{:S(2)}, u32[]{:S(2)}) collective-permute-start(bf16[640,2048]{1,0:T(8,128)(2,1)} %all-gather.2.cloned.1.call-done), channel_id=1, source_target_pairs={{0,2},{1,3},{2,0},{3,1},{4,6},{5,7},{6,4},{7,5},{8,10},{9,11},{10,... | collective-permute-start | bytes 7864328 | tf_op jit(solution)/shard_map/ppermute | solution.py:20
  121.6 84.0 %collective-permute-start.10 = (bf16[640,2048]{1,0:T(8,128)(2,1)}, bf16[640,2048]{1,0:T(8,128)(2,1)}, u32[]{:S(2)}, u32[]{:S(2)}) collective-permute-start(bf16[640,2048]{1,0:T(8,128)(2,1)} %all-gather.2.cloned.1.call-done), channel_id=1, source_target_pairs={{0,1},{1,0},{2,3},{3,2},{4,5},{5,4},{6,7},{7,6},{8,9},{9,8},{10,11... | collective-permute-start | bytes 7864328 | tf_op jit(solution)/shard_map/ppermute | solution.py:20
  169.1 40.9 %collective-permute-start.14 = (bf16[640,2048]{1,0:T(8,128)(2,1)}, bf16[640,2048]{1,0:T(8,128)(2,1)}, u32[]{:S(2)}, u32[]{:S(2)}) collective-permute-start(bf16[640,2048]{1,0:T(8,128)(2,1)} %collective-permute-done.12), channel_id=1, source_target_pairs={{0,1},{1,0},{2,3},{3,2},{4,5},{5,4},{6,7},{7,6},{8,9},{9,8},{10,11... | collective-permute-start | bytes 7864328 | tf_op jit(solution)/shard_map/ppermute | solution.py:20
  169.1 2.4 copy-start
  169.4 39.8 %collective-permute-start.13 = (bf16[640,512]{1,0:T(8,128)(2,1)S(1)}, bf16[640,512]{1,0:T(8,128)(2,1)S(1)}, u32[]{:S(2)}, u32[]{:S(2)}) collective-permute-start(bf16[640,512]{1,0:T(8,128)(2,1)S(1)} %get-tuple-element.11), channel_id=1, source_target_pairs={{0,3},{1,2},{2,1},{3,0},{4,7},{5,6},{6,5},{7,4},{8,11},{9,10},{10,... | collective-permute-start | bytes 1966088 | tf_op jit(solution)/shard_map/ppermute | solution.py:20
  171.0 29.5 %collective-permute-start.11 = (bf16[640,512]{1,0:T(8,128)(2,1)S(1)}, bf16[640,512]{1,0:T(8,128)(2,1)S(1)}, u32[]{:S(2)}, u32[]{:S(2)}) collective-permute-start(bf16[640,512]{1,0:T(8,128)(2,1)S(1)} %get-tuple-element.12), channel_id=1, source_target_pairs={{0,2},{1,3},{2,0},{3,1},{4,6},{5,7},{6,4},{7,5},{8,10},{9,11},{10,... | collective-permute-start | bytes 1966088 | tf_op jit(solution)/shard_map/ppermute | solution.py:20
  171.6 34.0 %collective-permute-start.9 = (bf16[640,512]{1,0:T(8,128)(2,1)S(1)}, bf16[640,512]{1,0:T(8,128)(2,1)S(1)}, u32[]{:S(2)}, u32[]{:S(2)}) collective-permute-start(bf16[640,512]{1,0:T(8,128)(2,1)S(1)} %get-tuple-element.13), channel_id=1, source_target_pairs={{0,1},{1,0},{2,3},{3,2},{4,5},{5,4},{6,7},{7,6},{8,9},{9,8},{10,11... | collective-permute-start | bytes 1966088 | tf_op jit(solution)/shard_map/ppermute | solution.py:20
  200.5 58.6 %collective-permute-start.4 = (f32[640,1024]{0,1:T(8,128)}, f32[640,1024]{0,1:T(8,128)}, u32[]{:S(2)}, u32[]{:S(2)}) collective-permute-start(f32[640,1024]{0,1:T(8,128)} %fusion.5), channel_id=1, source_target_pairs={{0,4},{4,0},{1,5},{5,1},{2,6},{6,2},{3,7},{7,3},{8,12},{12,8},{9,1... | collective-permute-start | bytes 7864328 | tf_op jit(solution)/shard_map/ppermute | solution.py:20
  209.2 0.8 copy-start.3
  214.5 44.6 %copy-start.1 = (bf16[640,2048]{1,0:T(8,128)(2,1)S(1)}, bf16[640,2048]{1,0:T(8,128)(2,1)}, u32[]{:S(2)}) copy-start(bf16[640,2048]{1,0:T(8,128)(2,1)} %all-gather.2.cloned.1.call-done) | copy-start | bytes 7864324
  228.8 54.9 %collective-permute-start.16 = (bf16[512,2048]{1,0:T(8,128)(2,1)}, bf16[512,2048]{1,0:T(8,128)(2,1)}, u32[]{:S(2)}, u32[]{:S(2)}) collective-permute-start(bf16[512,2048]{1,0:T(8,128)(2,1)} %get-tuple-element.7), channel_id=1, source_target_pairs={{0,2},{1,3},{2,0},{3,1},{4,6},{5,7},{6,4},{7,5},{8,10},{9,11},{10,... | collective-permute-start | bytes 6291464 | tf_op jit(solution)/shard_map/ppermute | solution.py:20
  230.3 112.9 %collective-permute-start.15 = (bf16[512,2048]{1,0:T(8,128)(2,1)}, bf16[512,2048]{1,0:T(8,128)(2,1)}, u32[]{:S(2)}, u32[]{:S(2)}) collective-permute-start(bf16[512,2048]{1,0:T(8,128)(2,1)} %get-tuple-element.7), channel_id=1, source_target_pairs={{0,1},{1,0},{2,3},{3,2},{4,5},{5,4},{6,7},{7,6},{8,9},{9,8},{10,11... | collective-permute-start | bytes 6291464 | tf_op jit(solution)/shard_map/ppermute | solution.py:20
  267.9 18.0 %collective-permute-start.7 = (bf16[160,1024]{0,1:T(8,128)(2,1)}, bf16[160,1024]{0,1:T(8,128)(2,1)}, u32[]{:S(2)}, u32[]{:S(2)}) collective-permute-start(bf16[160,1024]{0,1:T(8,128)(2,1)} %get-tuple-element.20), channel_id=1, source_target_pairs={{0,24},{8,16},{16,8},{24,0},{1,25},{9,17},{17,9},{25,1},{2,26},{10... | collective-permute-start | bytes 983048 | tf_op jit(solution)/shard_map/ppermute | solution.py:20
  268.2 48.8 %collective-permute-start.6 = (bf16[160,1024]{0,1:T(8,128)(2,1)}, bf16[160,1024]{0,1:T(8,128)(2,1)}, u32[]{:S(2)}, u32[]{:S(2)}) collective-permute-start(bf16[160,1024]{0,1:T(8,128)(2,1)} %get-tuple-element.21), channel_id=1, source_target_pairs={{0,16},{8,24},{16,0},{24,8},{1,17},{9,25},{17,1},{25,9},{2,18},{10... | collective-permute-start | bytes 983048 | tf_op jit(solution)/shard_map/ppermute | solution.py:20
  283.7 35.2 %collective-permute-start.5 = (bf16[160,1024]{0,1:T(8,128)(2,1)}, bf16[160,1024]{0,1:T(8,128)(2,1)}, u32[]{:S(2)}, u32[]{:S(2)}) collective-permute-start(bf16[160,1024]{0,1:T(8,128)(2,1)} %get-tuple-element.22), channel_id=1, source_target_pairs={{0,8},{8,0},{16,24},{24,16},{1,9},{9,1},{17,25},{25,17},{2,10},{10... | collective-permute-start | bytes 983048 | tf_op jit(solution)/shard_map/ppermute | solution.py:20
  283.7 68.1 %collective-permute-start.17 = (bf16[512,2048]{1,0:T(8,128)(2,1)}, bf16[512,2048]{1,0:T(8,128)(2,1)S(1)}, u32[]{:S(2)}, u32[]{:S(2)}) collective-permute-start(bf16[512,2048]{1,0:T(8,128)(2,1)} %collective-permute-done.16), channel_id=1, source_target_pairs={{0,1},{1,0},{2,3},{3,2},{4,5},{5,4},{6,7},{7,6},{8,9},{9,8},{10,11... | collective-permute-start | bytes 6291464 | tf_op jit(solution)/shard_map/ppermute | solution.py:20
  324.2 15.8 %collective-permute-start.8 = (bf16[320,1024]{1,0:T(8,128)(2,1)S(1)}, bf16[320,1024]{1,0:T(8,128)(2,1)S(1)}, u32[]{:S(2)}, u32[]{:S(2)}) collective-permute-start(bf16[320,1024]{1,0:T(8,128)(2,1)S(1)} %get-tuple-element.18), channel_id=1, source_target_pairs={{0,4},{4,0},{1,5},{5,1},{2,6},{6,2},{3,7},{7,3},{8,12},{12,8},{9,1... | collective-permute-start | bytes 1966088 | tf_op jit(solution)/shard_map/ppermute | solution.py:20
Sparse Core Ops, SparseCore 0:
  9.5 79.2 all-gather.1
  121.7 104.5 reduce-scatter.1
where the time goes:
time: 361 us; the launch traced here: 360 us
  waiting for transfers between devices  228 us (63%)
  matrix products  48.8 us (14%)
  local copies, waits for them, and re-layouts  35.5 us (10%)
  starting transfers between devices  31.8 us (9%)
  between operations  14.3 us (4%)
    ppermute x18, waiting for transfers between devices, swap(): return lax.ppermute(value, axis, [(i, i ^ step) for i in range(size)])  227 us
    ppermute x18, starting transfers between devices, swap(): return lax.ppermute(value, axis, [(i, i ^ step) for i in range(size)])  31.7 us
    dot_general x4, matrix products, step(): lax.dot_general(slab, other_cotangent, (((0,), (0,)), ((), ())), preferre...  25.4 us
    dynamic_update_slice x13, local copies, waits for them, and re-layouts, in_order(): lax.dynamic_update_slice_in_dim(whole, piece, (me ^ step) * size, dim)  15.5 us
    dot_general x2, matrix products, step(): lax.dot_general(line_cotangent, panel, (((1,), (1,)), ((), ())), preferre...  13.8 us
    dot_general x1, matrix products, step(): jnp.dot(line_tokens, weight, preferred_element_type=jnp.float32)  9.51 us
  transfers between devices with their start and end apart: 20, of which 8 were waited for; matrix products, arithmetic and copies ran while one was open for 23% of the time, Pallas kernels for 0%

commit v1 on v0

--- a/solution.py
+++ b/solution.py
@@ -25,7 +25,9 @@
     for step in range(1, lax.axis_size(axis)):
         top = 1 << (step.bit_length() - 1)
         low = step & -step
-        pieces.append(swap(pieces[step - low], axis, low) if step != top else swap(value, axis, step))
+        pieces.append(
+            swap(value, axis, step) if step == top else swap(pieces[step - low], axis, low)
+        )
     return pieces
 
 
@@ -90,7 +92,8 @@
     step_value = new_first / bias_one / (jnp.sqrt(new_second / bias_two) + adam_eps)
     new_master = master - learn_rate * (step_value + decay_rate * master)
     shard_weight = new_master.astype(jnp.bfloat16)
-    new_weight = in_order(spread(shard_weight, "depth"), "depth", 0)
+    weight_pieces = spread(shard_weight, "depth")
+    new_weight = in_order(weight_pieces, "depth", 0)
     return (queries, token_grad, new_master, new_first, new_second, new_weight)
 
 

time: 361 us -> 361 us (level)
  no operation moved by 1% of the time
where the time goes in v1:
time: 361 us; the launch traced here: 360 us
  waiting for transfers between devices  228 us (63%)
  matrix products  48.8 us (14%)
  local copies, waits for them, and re-layouts  35.5 us (10%)
  starting transfers between devices  31.8 us (9%)
  between operations  14.3 us (4%)
    ppermute x18, waiting for transfers between devices, swap(): return lax.ppermute(value, axis, [(i, i ^ step) for i in range(size)])  227 us
    ppermute x18, starting transfers between devices, swap(): return lax.ppermute(value, axis, [(i, i ^ step) for i in range(size)])  31.7 us
    dot_general x4, matrix products, step(): lax.dot_general(slab, other_cotangent, (((0,), (0,)), ((), ())), preferre...  25.4 us
    dynamic_update_slice x13, local copies, waits for them, and re-layouts, in_order(): lax.dynamic_update_slice_in_dim(whole, piece, (me ^ step) * size, dim)  15.5 us
    dot_general x2, matrix products, step(): lax.dot_general(line_cotangent, panel, (((1,), (1,)), ((), ())), preferre...  13.8 us
    dot_general x1, matrix products, step(): jnp.dot(line_tokens, weight, preferred_element_type=jnp.float32)  9.51 us
  transfers between devices with their start and end apart: 20, of which 8 were waited for; matrix products, arithmetic and copies ran while one was open for 23% of the time, Pallas kernels for 0%

profile of v1, /device:TPU:0, one launch (start us, length us, event | category | flops | bytes accessed | tf_op | source)
XLA Modules:
  0.0 360.1 jit_solution(10849362117627997346)
XLA Ops:
  8.0 3.0 collective-permute-start
  11.4 28.5 %collective-permute-done = bf16[160,4096]{1,0:T(8,128)(2,1)S(1)} collective-permute-done((bf16[160,4096]{1,0:T(8,128)(2,1)}, bf16[160,4096]{1,0:T(8,128)(2,1)S(1)}, u32[]{:S(2)}, u32[]{:S(2)}) %collective-permute-start) | collective-permute-done | bytes 1310752 | tf_op jit(solution)/shard_map/ppermute | solution.py:20
  41.7 1.8 collective-permute-start.1
  43.6 2.6 collective-permute-start.2
  46.2 47.0 %collective-permute-done.1 = bf16[160,2048]{1,0:T(8,128)(2,1)} collective-permute-done((bf16[160,2048]{1,0:T(8,128)(2,1)}, bf16[160,2048]{1,0:T(8,128)(2,1)}, u32[]{:S(2)}, u32[]{:S(2)}) %collective-permute-start.1) | collective-permute-done | bytes 655392 | tf_op jit(solution)/shard_map/ppermute | solution.py:20
  95.4 13.9 %collective-permute-done.3 = bf16[160,2048]{1,0:T(8,128)(2,1)} collective-permute-done((bf16[160,2048]{1,0:T(8,128)(2,1)S(1)}, bf16[160,2048]{1,0:T(8,128)(2,1)}, u32[]{:S(2)}, u32[]{:S(2)}) %collective-permute-start.3) | collective-permute-done | bytes 655392 | tf_op jit(solution)/shard_map/ppermute | solution.py:20
  110.5 1.5 collective-permute-start.12
  112.0 9.5 %fusion.15 = f32[640,2048]{1,0:T(8,128)} fusion(bf16[640,2048]{1,0:T(8,128)(2,1)S(1)} %constant_dynamic-update-slice_fusion.8, bf16[2048,2048]{1,0:T(8,128)(2,1)} %param.7), kind=kOutput, calls=%fused_computation.43 | convolution fusion | flops 5368709120 | bytes 16252928 | tf_op jit(solution)/shard_map/dot_general | solution.py:73
  121.6 47.5 %collective-permute-done.12 = bf16[640,2048]{1,0:T(8,128)(2,1)} collective-permute-done((bf16[640,2048]{1,0:T(8,128)(2,1)}, bf16[640,2048]{1,0:T(8,128)(2,1)}, u32[]{:S(2)}, u32[]{:S(2)}) %collective-permute-start.12) | collective-permute-done | bytes 2621472 | tf_op jit(solution)/shard_map/ppermute | solution.py:20
  169.4 1.7 collective-permute-start.13
  171.6 7.3 %fusion.5 = f32[640,1024]{0,1:T(8,128)} fusion(bf16[640,2048]{1,0:T(8,128)(2,1)S(1)} %copy-done, bf16[2048,2048]{1,0:T(8,128)(2,1)} %param.7, s32[]{:T(128)S(6)} %select_n.78), kind=kOutput, calls=%fused_computation.10 | convolution fusion | flops 2684354560 | bytes 9437188 | tf_op jit(solution)/shard_map/dot_general | solution.py:67
  178.8 3.9 %fusion.10 = f32[512,2048]{1,0:T(8,128)} fusion(bf16[640,2048]{1,0:T(8,128)(2,1)S(1)} %copy-done, bf16[640,2048]{1,0:T(8,128)(2,1)S(1)} %constant_dynamic-update-slice_fusion.8, s32[]{:T(128)S(6)} %select_n.82), kind=kOutput, calls=%fused_computation.12 | convolution fusion | flops 1342177280 | bytes 7471108 | tf_op jit(solution)/shard_map/dot_general | solution.py:86
  182.8 17.7 %collective-permute-done.11 = bf16[640,512]{1,0:T(8,128)(2,1)S(1)} collective-permute-done((bf16[640,512]{1,0:T(8,128)(2,1)S(1)}, bf16[640,512]{1,0:T(8,128)(2,1)S(1)}, u32[]{:S(2)}, u32[]{:S(2)}) %collective-permute-start.11) | collective-permute-done | bytes 655392 | tf_op jit(solution)/shard_map/ppermute | solution.py:20
  202.0 3.6 fusion.17
  205.6 3.6 fusion.16
  210.0 4.5 %broadcast_in_dim.11 = bf16[2048,2048]{1,0:T(8,128)(2,1)} broadcast(bf16[]{:T(256)} %constant.26.clone.1), dimensions={} | broadcast | bytes 8388610 | tf_op jit(solution)/shard_map/broadcast_in_dim | solution.py:48
  214.5 14.3 %constant_dynamic-update-slice_fusion.1 = (bf16[2048,2048]{1,0:T(8,128)(2,1)}, bf16[512,2048]{1,0:T(8,128)(2,1)}, f32[512,2048]{1,0:T(8,128)}, f32[512,2048]{1,0:T(8,128)}, f32[512,2048]{1,0:T(8,128)}) fusion(bf16[2048,2048]{1,0:T(8,128)(2,1)} %broadcast_in_dim.11, s32[]{:T(128)S(6)} %select_n.82, f32[512,2048]{1,0:T(8,128)} %param.9, ...), kind=kOutput, calls=%fused_computation.16 | convolution fusion | flops 1363148800 | bytes 45219844 | tf_op jit(solution)/shard_map/dot_general | solution.py:86
  228.8 1.5 collective-permute-start.16
  230.3 28.8 %collective-permute-done.4 = f32[640,1024]{0,1:T(8,128)} collective-permute-done((f32[640,1024]{0,1:T(8,128)}, f32[640,1024]{0,1:T(8,128)}, u32[]{:S(2)}, u32[]{:S(2)}) %collective-permute-start.4) | collective-permute-done | bytes 2621472 | tf_op jit(solution)/shard_map/ppermute | solution.py:20
  259.1 6.5 %fusion.4 = bf16[640,1024]{0,1:T(8,128)(2,1)S(1)} fusion(f32[640,1024]{0,1:T(8,128)} %collective-permute-done.4, bf16[640,2048]{1,0:T(8,128)(2,1)S(1)} %copy-done.1, bf16[2048,2048]{1,0:T(8,128)(2,1)} %param.7, s32[]{:T(128)S(6)} %select_n.79), kind=kOutput, calls=%fused_computation.9 | convolution fusion | flops 2685665280 | bytes 10747908 | tf_op jit(solution)/shard_map/dot_general | solution.py:67
  265.7 2.2 constant_dynamic-slice_fusion.4
  268.2 15.5 %collective-permute-start.6 = (bf16[160,1024]{0,1:T(8,128)(2,1)}, bf16[160,1024]{0,1:T(8,128)(2,1)}, u32[]{:S(2)}, u32[]{:S(2)}) collective-permute-start(bf16[160,1024]{0,1:T(8,128)(2,1)} %get-tuple-element.21), channel_id=1, source_target_pairs={{0,16},{8,24},{16,0},{24,8},{1,17},{9,25},{17,1},{25,9},{2,18},{10... | collective-permute-start | bytes 983048 | tf_op jit(solution)/shard_map/ppermute | solution.py:20
  285.9 2.0 copy.23
  287.8 29.2 %collective-permute-done.6 = bf16[160,1024]{0,1:T(8,128)(2,1)} collective-permute-done((bf16[160,1024]{0,1:T(8,128)(2,1)}, bf16[160,1024]{0,1:T(8,128)(2,1)}, u32[]{:S(2)}, u32[]{:S(2)}) %collective-permute-start.6) | collective-permute-done | bytes 327712 | tf_op jit(solution)/shard_map/ppermute | solution.py:20
  317.0 1.9 copy.22
  319.0 1.9 copy.21
  324.2 1.5 collective-permute-start.8
  325.7 14.3 %collective-permute-done.8 = bf16[320,1024]{1,0:T(8,128)(2,1)S(1)} collective-permute-done((bf16[320,1024]{1,0:T(8,128)(2,1)S(1)}, bf16[320,1024]{1,0:T(8,128)(2,1)S(1)}, u32[]{:S(2)}, u32[]{:S(2)}) %collective-permute-start.8) | collective-permute-done | bytes 655392 | tf_op jit(solution)/shard_map/ppermute | solution.py:20
  341.4 1.8 reshape.19
  343.2 3.2 constant_dynamic-update-slice_fusion
  346.4 3.2 constant_dynamic-update-slice_fusion.11
  349.6 2.2 convert_element_type.9
  (54 shorter events, 18.1 us)
Async XLA Ops:
  7.2 4.1 %copy-start.2 = (bf16[160,4096]{1,0:T(8,128)(2,1)S(1)}, bf16[160,4096]{1,0:T(8,128)(2,1)}, u32[]{:S(2)}) copy-start(bf16[160,4096]{1,0:T(8,128)(2,1)} %param.6) | copy-start | bytes 3932164
  7.2 103.3 %all-gather.2.cloned.1.call-start = ((), (), s32[]{:S(2)}) async-start(), calls=%async_computation.2 | async-start | bytes 3276800 | tf_op jit(solution)/shard_map/all_gather | solution.py:61
  7.9 341.7 %reduce-scatter.2.cloned.1.call-start = ((), (), s32[]{:S(2)}) async-start(), calls=%async_computation.1 | async-start | bytes 6553600 | tf_op jit(solution)/shard_map/reduce_scatter | solution.py:74
  8.0 32.0 %collective-permute-start = (bf16[160,4096]{1,0:T(8,128)(2,1)}, bf16[160,4096]{1,0:T(8,128)(2,1)S(1)}, u32[]{:S(2)}, u32[]{:S(2)}) collective-permute-start(bf16[160,4096]{1,0:T(8,128)(2,1)} %param.6), channel_id=1, source_target_pairs={{0,4},{4,0},{1,5},{5,1},{2,6},{6,2},{3,7},{7,3},{8,12},{12,8},{9,1... | collective-permute-start | bytes 3932168 | tf_op jit(solution)/shard_map/ppermute | solution.py:20
  41.7 51.4 %collective-permute-start.1 = (bf16[160,2048]{1,0:T(8,128)(2,1)}, bf16[160,2048]{1,0:T(8,128)(2,1)}, u32[]{:S(2)}, u32[]{:S(2)}) collective-permute-start(bf16[160,2048]{1,0:T(8,128)(2,1)} %get-tuple-element.16), channel_id=1, source_target_pairs={{0,8},{8,0},{16,24},{24,16},{1,9},{9,1},{17,25},{25,17},{2,10},{10... | collective-permute-start | bytes 1966088 | tf_op jit(solution)/shard_map/ppermute | solution.py:20
  43.6 50.7 %collective-permute-start.2 = (bf16[160,2048]{1,0:T(8,128)(2,1)}, bf16[160,2048]{1,0:T(8,128)(2,1)}, u32[]{:S(2)}, u32[]{:S(2)}) collective-permute-start(bf16[160,2048]{1,0:T(8,128)(2,1)} %get-tuple-element.15), channel_id=1, source_target_pairs={{0,16},{8,24},{16,0},{24,8},{1,17},{9,25},{17,1},{25,9},{2,18},{10... | collective-permute-start | bytes 1966088 | tf_op jit(solution)/shard_map/ppermute | solution.py:20
  46.2 63.1 %collective-permute-start.3 = (bf16[160,2048]{1,0:T(8,128)(2,1)S(1)}, bf16[160,2048]{1,0:T(8,128)(2,1)}, u32[]{:S(2)}, u32[]{:S(2)}) collective-permute-start(bf16[160,2048]{1,0:T(8,128)(2,1)S(1)} %get-tuple-element.14), channel_id=1, source_target_pairs={{0,24},{8,16},{16,8},{24,0},{1,25},{9,17},{17,9},{25,1},{2,26},{10... | collective-permute-start | bytes 1966088 | tf_op jit(solution)/shard_map/ppermute | solution.py:20
  110.5 58.6 %collective-permute-start.12 = (bf16[640,2048]{1,0:T(8,128)(2,1)}, bf16[640,2048]{1,0:T(8,128)(2,1)}, u32[]{:S(2)}, u32[]{:S(2)}) collective-permute-start(bf16[640,2048]{1,0:T(8,128)(2,1)} %all-gather.2.cloned.1.call-done), channel_id=1, source_target_pairs={{0,2},{1,3},{2,0},{3,1},{4,6},{5,7},{6,4},{7,5},{8,10},{9,11},{10,... | collective-permute-start | bytes 7864328 | tf_op jit(solution)/shard_map/ppermute | solution.py:20
  121.6 84.0 %collective-permute-start.10 = (bf16[640,2048]{1,0:T(8,128)(2,1)}, bf16[640,2048]{1,0:T(8,128)(2,1)}, u32[]{:S(2)}, u32[]{:S(2)}) collective-permute-start(bf16[640,2048]{1,0:T(8,128)(2,1)} %all-gather.2.cloned.1.call-done), channel_id=1, source_target_pairs={{0,1},{1,0},{2,3},{3,2},{4,5},{5,4},{6,7},{7,6},{8,9},{9,8},{10,11... | collective-permute-start | bytes 7864328 | tf_op jit(solution)/shard_map/ppermute | solution.py:20
  169.1 40.9 %collective-permute-start.14 = (bf16[640,2048]{1,0:T(8,128)(2,1)}, bf16[640,2048]{1,0:T(8,128)(2,1)}, u32[]{:S(2)}, u32[]{:S(2)}) collective-permute-start(bf16[640,2048]{1,0:T(8,128)(2,1)} %collective-permute-done.12), channel_id=1, source_target_pairs={{0,1},{1,0},{2,3},{3,2},{4,5},{5,4},{6,7},{7,6},{8,9},{9,8},{10,11... | collective-permute-start | bytes 7864328 | tf_op jit(solution)/shard_map/ppermute | solution.py:20
  169.1 2.4 copy-start
  169.4 39.8 %collective-permute-start.13 = (bf16[640,512]{1,0:T(8,128)(2,1)S(1)}, bf16[640,512]{1,0:T(8,128)(2,1)S(1)}, u32[]{:S(2)}, u32[]{:S(2)}) collective-permute-start(bf16[640,512]{1,0:T(8,128)(2,1)S(1)} %get-tuple-element.11), channel_id=1, source_target_pairs={{0,3},{1,2},{2,1},{3,0},{4,7},{5,6},{6,5},{7,4},{8,11},{9,10},{10,... | collective-permute-start | bytes 1966088 | tf_op jit(solution)/shard_map/ppermute | solution.py:20
  171.0 29.5 %collective-permute-start.11 = (bf16[640,512]{1,0:T(8,128)(2,1)S(1)}, bf16[640,512]{1,0:T(8,128)(2,1)S(1)}, u32[]{:S(2)}, u32[]{:S(2)}) collective-permute-start(bf16[640,512]{1,0:T(8,128)(2,1)S(1)} %get-tuple-element.12), channel_id=1, source_target_pairs={{0,2},{1,3},{2,0},{3,1},{4,6},{5,7},{6,4},{7,5},{8,10},{9,11},{10,... | collective-permute-start | bytes 1966088 | tf_op jit(solution)/shard_map/ppermute | solution.py:20
  171.6 34.0 %collective-permute-start.9 = (bf16[640,512]{1,0:T(8,128)(2,1)S(1)}, bf16[640,512]{1,0:T(8,128)(2,1)S(1)}, u32[]{:S(2)}, u32[]{:S(2)}) collective-permute-start(bf16[640,512]{1,0:T(8,128)(2,1)S(1)} %get-tuple-element.13), channel_id=1, source_target_pairs={{0,1},{1,0},{2,3},{3,2},{4,5},{5,4},{6,7},{7,6},{8,9},{9,8},{10,11... | collective-permute-start | bytes 1966088 | tf_op jit(solution)/shard_map/ppermute | solution.py:20
  200.5 58.6 %collective-permute-start.4 = (f32[640,1024]{0,1:T(8,128)}, f32[640,1024]{0,1:T(8,128)}, u32[]{:S(2)}, u32[]{:S(2)}) collective-permute-start(f32[640,1024]{0,1:T(8,128)} %fusion.5), channel_id=1, source_target_pairs={{0,4},{4,0},{1,5},{5,1},{2,6},{6,2},{3,7},{7,3},{8,12},{12,8},{9,1... | collective-permute-start | bytes 7864328 | tf_op jit(solution)/shard_map/ppermute | solution.py:20
  209.2 0.8 copy-start.3
  214.5 44.6 %copy-start.1 = (bf16[640,2048]{1,0:T(8,128)(2,1)S(1)}, bf16[640,2048]{1,0:T(8,128)(2,1)}, u32[]{:S(2)}) copy-start(bf16[640,2048]{1,0:T(8,128)(2,1)} %all-gather.2.cloned.1.call-done) | copy-start | bytes 7864324
  228.8 54.9 %collective-permute-start.16 = (bf16[512,2048]{1,0:T(8,128)(2,1)}, bf16[512,2048]{1,0:T(8,128)(2,1)}, u32[]{:S(2)}, u32[]{:S(2)}) collective-permute-start(bf16[512,2048]{1,0:T(8,128)(2,1)} %get-tuple-element.7), channel_id=1, source_target_pairs={{0,2},{1,3},{2,0},{3,1},{4,6},{5,7},{6,4},{7,5},{8,10},{9,11},{10,... | collective-permute-start | bytes 6291464 | tf_op jit(solution)/shard_map/ppermute | solution.py:20
  230.3 112.9 %collective-permute-start.15 = (bf16[512,2048]{1,0:T(8,128)(2,1)}, bf16[512,2048]{1,0:T(8,128)(2,1)}, u32[]{:S(2)}, u32[]{:S(2)}) collective-permute-start(bf16[512,2048]{1,0:T(8,128)(2,1)} %get-tuple-element.7), channel_id=1, source_target_pairs={{0,1},{1,0},{2,3},{3,2},{4,5},{5,4},{6,7},{7,6},{8,9},{9,8},{10,11... | collective-permute-start | bytes 6291464 | tf_op jit(solution)/shard_map/ppermute | solution.py:20
  267.9 18.0 %collective-permute-start.7 = (bf16[160,1024]{0,1:T(8,128)(2,1)}, bf16[160,1024]{0,1:T(8,128)(2,1)}, u32[]{:S(2)}, u32[]{:S(2)}) collective-permute-start(bf16[160,1024]{0,1:T(8,128)(2,1)} %get-tuple-element.20), channel_id=1, source_target_pairs={{0,24},{8,16},{16,8},{24,0},{1,25},{9,17},{17,9},{25,1},{2,26},{10... | collective-permute-start | bytes 983048 | tf_op jit(solution)/shard_map/ppermute | solution.py:20
  268.2 48.8 %collective-permute-start.6 = (bf16[160,1024]{0,1:T(8,128)(2,1)}, bf16[160,1024]{0,1:T(8,128)(2,1)}, u32[]{:S(2)}, u32[]{:S(2)}) collective-permute-start(bf16[160,1024]{0,1:T(8,128)(2,1)} %get-tuple-element.21), channel_id=1, source_target_pairs={{0,16},{8,24},{16,0},{24,8},{1,17},{9,25},{17,1},{25,9},{2,18},{10... | collective-permute-start | bytes 983048 | tf_op jit(solution)/shard_map/ppermute | solution.py:20
  283.7 35.2 %collective-permute-start.5 = (bf16[160,1024]{0,1:T(8,128)(2,1)}, bf16[160,1024]{0,1:T(8,128)(2,1)}, u32[]{:S(2)}, u32[]{:S(2)}) collective-permute-start(bf16[160,1024]{0,1:T(8,128)(2,1)} %get-tuple-element.22), channel_id=1, source_target_pairs={{0,8},{8,0},{16,24},{24,16},{1,9},{9,1},{17,25},{25,17},{2,10},{10... | collective-permute-start | bytes 983048 | tf_op jit(solution)/shard_map/ppermute | solution.py:20
  283.7 68.1 %collective-permute-start.17 = (bf16[512,2048]{1,0:T(8,128)(2,1)}, bf16[512,2048]{1,0:T(8,128)(2,1)S(1)}, u32[]{:S(2)}, u32[]{:S(2)}) collective-permute-start(bf16[512,2048]{1,0:T(8,128)(2,1)} %collective-permute-done.16), channel_id=1, source_target_pairs={{0,1},{1,0},{2,3},{3,2},{4,5},{5,4},{6,7},{7,6},{8,9},{9,8},{10,11... | collective-permute-start | bytes 6291464 | tf_op jit(solution)/shard_map/ppermute | solution.py:20
  324.2 15.8 %collective-permute-start.8 = (bf16[320,1024]{1,0:T(8,128)(2,1)S(1)}, bf16[320,1024]{1,0:T(8,128)(2,1)S(1)}, u32[]{:S(2)}, u32[]{:S(2)}) collective-permute-start(bf16[320,1024]{1,0:T(8,128)(2,1)S(1)} %get-tuple-element.18), channel_id=1, source_target_pairs={{0,4},{4,0},{1,5},{5,1},{2,6},{6,2},{3,7},{7,3},{8,12},{12,8},{9,1... | collective-permute-start | bytes 1966088 | tf_op jit(solution)/shard_map/ppermute | solution.py:20
Sparse Core Ops, SparseCore 0:
  9.5 79.2 all-gather.1
  121.7 104.5 reduce-scatter.1
